TPU v7x, 128 devices: a whole 4x4x4 slice. The times are simulated.
128 devices in a mesh: row: 8 (over y, core), col: 16 (over x, z).
Axes of the slice: x: 4, y: 4, z: 4, core: 2. Of those that a mesh axis runs over, the one named last changes fastest.
Arguments:
- theta: float32 [64, 256, 256], P('row', None, 'col'), may hold values from -6 to 6
- left_env: float32 [32, 32, 256, 256], P('row', 'col'), as said below
- right_env: float32 [8, 32, 256, 256], P(None, 'col'), as said below
- left_sector: int32 [64], replicated, may hold values from 0 to 31, as said below
- right_sector: int32 [64], P('row'), may hold values from 0 to 7
- term_on: int32 [64, 32], P('row', 'col'), may hold values 0 or 1
- left_size: int32 [32], replicated, may hold values from 1 to 256, 5120 in all
- right_size: int32 [8], replicated, may hold values from 1 to 256, 1280 in all
Outputs:
- new_theta: float32 [64, 256, 256], P('row', None, 'col')
- energy: float32 [], replicated
Inputs may be any that keep to these rules, and one draw needn't show every extreme that they name: `left_sector`: left sector s belongs to row s // 4. Block k belongs to row k // 8. The 8 blocks of one row name distinct left sectors; they name either none or exactly 2 sectors belonging to any one row, and the blocks of every row name 2 sectors belonging to one common row. `left_env`: each tile is symmetric in its last two dimensions. `right_env`: each tile is symmetric in its last two dimensions.
All inputs are finite; a program needn't handle non-finite values. No bound on the sum of `term_on` on one device may be relied on, other than what follows from the above.
Results may differ from a plain program's by a relative error of at most 0.0001.
Values sent between devices are 32-bit elements; how exact they have to be, the bound alone decides.
No kernel may reach another device: no remote copies, remote signals or barrier semaphores. Data moves between devices by JAX's collectives and lax.ppermute only.
A program may use at most 128 MiB of HBM per device.

v0:
```python
import jax
import jax.numpy as jnp
from jax import lax
from jax.sharding import PartitionSpec as P

ITERS = 2
highest = lax.Precision.HIGHEST


def lookup(small_table, index_list):
    slot_hits = index_list[:, None] == jnp.arange(small_table.shape[0], dtype=jnp.int32)[None, :]
    return jnp.sum(jnp.where(slot_hits, small_table[None, :], 0), axis=1)


def tile_masks(left_ids, right_ids, left_size, right_size, tile_size, offset, span_cols):
    rows_live = lookup(left_size, left_ids)
    cols_live = lookup(right_size, right_ids)
    row_mask = (jnp.arange(tile_size, dtype=jnp.int32)[None, :] < rows_live[:, None]).astype(
        jnp.float32
    )
    col_mask = (
        (offset + jnp.arange(span_cols, dtype=jnp.int32))[None, :] < cols_live[:, None]
    ).astype(jnp.float32)
    return row_mask[:, :, None] * col_mask[:, None, :]


def local(theta, left_env, right_env, left_sector, right_sector, term_on, left_size, right_size):
    row_count = lax.axis_size("row")
    blocks, tile_size, thin_cols = theta.shape
    local_sectors = left_env.shape[0]
    capacity = max(2, 2 * blocks // row_count)
    row_index = lax.axis_index("row")
    col_index = lax.axis_index("col")
    own_left = lax.dynamic_slice_in_dim(left_sector, row_index * blocks, blocks)
    offset = col_index * thin_cols
    span_cols = theta.shape[2]
    start_mask = tile_masks(
        own_left, right_sector, left_size, right_size, tile_size, offset, span_cols
    )
    start_vec = theta * start_mask
    senders = row_index * local_sectors + jnp.arange(local_sectors, dtype=jnp.int32)
    wanted = left_sector.reshape(row_count, blocks)
    used_flag = jnp.any(wanted[:, :, None] == senders[None, None, :], axis=1)
    used_count = used_flag.astype(jnp.int32)
    before = jnp.cumsum(used_count, axis=1) - used_count
    pick_flag = used_flag[:, None, :] & (
        before[:, None, :] == jnp.arange(capacity, dtype=jnp.int32)[None, :, None]
    )
    filled = jnp.any(pick_flag, axis=2).reshape(-1)
    local_index = jnp.sum(
        jnp.where(pick_flag, jnp.arange(local_sectors, dtype=jnp.int32)[None, None, :], 0), axis=2
    ).reshape(-1)
    outgoing = (
        jnp.take(left_env, local_index, axis=0) * filled.astype(jnp.float32)[:, None, None, None]
    )
    arrived = lax.all_to_all(outgoing, "row", split_axis=0, concat_axis=0, tiled=True)
    every_sector = jnp.arange(row_count * local_sectors, dtype=jnp.int32)
    needed = (
        jnp.any(own_left[:, None] == every_sector[None, :], axis=0)
        .astype(jnp.int32)
        .reshape(row_count, local_sectors)
    )
    order_rank = (jnp.cumsum(needed, axis=1) - needed).reshape(-1)
    position = own_left // local_sectors * capacity + lookup(order_rank, own_left)
    left_pick = jnp.take(arrived, position, axis=0)
    right_pick = jnp.take(right_env, right_sector, axis=0)
    weights = term_on.astype(jnp.float32)

    def contract(full_vector):
        middle = (
            jnp.einsum("swia,sab->swib", left_pick, full_vector, precision=highest)
            * weights[:, :, None, None]
        )
        return jnp.einsum("swib,swjb->sij", middle, right_pick, precision=highest)

    def operate(vector):
        full_vector = lax.all_gather(vector, "col", axis=2, tiled=True)
        total_sum = lax.psum_scatter(contract(full_vector), "col", scatter_dimension=2, tiled=True)
        return total_sum * start_mask

    def combine(values):
        reduced = lax.psum(values, ("row", "col"))
        return reduced

    image_vec = operate(start_vec)
    norm_sq, correlation = combine((jnp.sum(start_vec * start_vec), jnp.sum(start_vec * image_vec)))
    inv_norm = 1.0 / jnp.sqrt(norm_sq)
    basis_vec = start_vec * inv_norm
    applied = image_vec * inv_norm
    ritz_value = correlation / norm_sq
    for turn_index in range(ITERS):
        residual = applied - ritz_value * basis_vec
        (res_sq,) = combine((jnp.sum(residual * residual),))
        length = jnp.sqrt(res_sq)
        fresh_vec = residual / length
        fresh_applied = operate(fresh_vec)
        (curvature,) = combine((jnp.sum(fresh_vec * fresh_applied),))
        half_gap = 0.5 * (ritz_value - curvature)
        root_term = jnp.sqrt(half_gap * half_gap + res_sq)
        lowest = 0.5 * (ritz_value + curvature) - root_term
        first_coef = curvature - lowest
        pair_norm = jnp.sqrt(first_coef * first_coef + res_sq)
        basis_vec = (first_coef * basis_vec - length * fresh_vec) / pair_norm
        applied = (first_coef * applied - length * fresh_applied) / pair_norm
        ritz_value = lowest
    total_entries = blocks * row_count * tile_size * tile_size
    output = basis_vec * jnp.sqrt(jnp.float32(total_entries))
    return (output, ritz_value)


def solution(mesh):
    placed = (
        P("row", None, "col"),
        P("row", "col", None, None),
        P(None, "col", None, None),
        P(),
        P("row"),
        P("row", "col"),
        P(),
        P(),
    )
    return jax.shard_map(
        local, mesh=mesh, in_specs=placed, out_specs=(P("row", None, "col"), P()), check_vma=False
    )
```

profile of v0, /device:TPU:1, one launch (start us, length us, event | category | flops | bytes accessed | tf_op | source)
XLA Modules:
  0.0 820.7 jit_solution(7117098073512323360)
XLA Ops:
  7.2 0.9 eq.29
  8.9 4.3 gather_fusion
  13.2 7.9 select_multiply_fusion
  21.1 6.4 all-to-all-start
  28.6 0.7 multiply_multiply_fusion.3
  29.5 4.9 gather_fusion.2
  34.5 86.8 %all-to-all-done = f32[16,2,256,256]{3,2,1,0:T(8,128)} async-done(((f32[16,2,256,256]{3,2,1,0:T(8,128)}), f32[16,2,256,256]{3,2,1,0:T(8,128)}, u32[]{:S(2)}, u32[]{:S(2)}) %all-to-all-start) | async-done | bytes 8388640 | tf_op jit(solution)/shard_map/all_to_all | solution.py:56
  121.4 6.2 gather_fusion.1
  127.6 6.8 fusion.13
  134.4 5.9 fusion.33
  140.3 73.6 %reduce-scatter.4.cloned.1.call-done = f32[8,256,16]{1,2,0:T(8,128)} async-done(((f32[8,256,256]{1,2,0:T(8,128)}), f32[8,256,16]{1,2,0:T(8,128)}) %reduce-scatter.4.cloned.1.call-update) | async-done | bytes 131088 | tf_op jit(solution)/shard_map/reduce_scatter | solution.py:78
  213.9 1.6 multiply_reduce_fusion.4
  215.6 65.9 %all-reduce = (f32[]{:T(128)}, f32[]{:T(128)}) all-reduce(f32[]{:T(128)} %get-tuple-element.3, f32[]{:T(128)} %get-tuple-element.2), channel_id=1, replica_groups=mesh['row'=8,'col'=16] {'row','col'}, use_global_device_ids=true, to_apply=%region_13.14 | all-reduce | flops 2 | bytes 16 | tf_op jit(solution)/shard_map/psum | solution.py:82
  283.5 1.6 multiply_reduce_fusion.2
  285.1 62.7 %psum.44 = f32[]{:T(128)} all-reduce(f32[]{:T(128)} %multiply_reduce_fusion.2), channel_id=1, replica_groups=mesh['row'=8,'col'=16] {'row','col'}, use_global_device_ids=true, to_apply=%region_15.16 | all-reduce | flops 1 | bytes 8 | tf_op jit(solution)/shard_map/psum | solution.py:82
  348.5 1.7 broadcast_divide_fusion.1
  350.2 41.4 %all-gather.6.cloned.1.call-done = f32[8,256,256]{1,2,0:T(8,128)} async-done(((f32[8,256,16]{1,2,0:T(8,128)}), f32[8,256,256]{1,2,0:T(8,128)}) %all-gather.6.cloned.1.call-update) | async-done | bytes 2097168 | tf_op jit(solution)/shard_map/all_gather | solution.py:77
  391.6 6.8 fusion.11
  398.5 5.9 fusion.38
  404.4 73.2 %reduce-scatter.6.cloned.1.call-done = f32[8,256,16]{1,2,0:T(8,128)} async-done(((f32[8,256,256]{1,2,0:T(8,128)}), f32[8,256,16]{1,2,0:T(8,128)}) %reduce-scatter.6.cloned.1.call-update) | async-done | bytes 131088 | tf_op jit(solution)/shard_map/reduce_scatter | solution.py:78
  477.6 1.6 multiply_reduce_fusion.1
  479.2 65.8 %psum.45 = f32[]{:T(128)} all-reduce(f32[]{:T(128)} %multiply_reduce_fusion.1), channel_id=1, replica_groups=mesh['row'=8,'col'=16] {'row','col'}, use_global_device_ids=true, to_apply=%region_18.19 | all-reduce | flops 1 | bytes 8 | tf_op jit(solution)/shard_map/psum | solution.py:82
  548.3 1.7 multiply_reduce_fusion
  550.0 62.5 %psum.46 = f32[]{:T(128)} all-reduce(f32[]{:T(128)} %get-tuple-element.8), channel_id=1, replica_groups=mesh['row'=8,'col'=16] {'row','col'}, use_global_device_ids=true, to_apply=%region_20.21 | all-reduce | flops 1 | bytes 8 | tf_op jit(solution)/shard_map/psum | solution.py:82
  613.2 0.7 broadcast_divide_fusion
  614.2 41.2 %all-gather.8.cloned.1.call-done = f32[8,256,256]{1,2,0:T(8,128)} async-done(((f32[8,256,16]{1,2,0:T(8,128)}), f32[8,256,256]{1,2,0:T(8,128)}) %all-gather.8.cloned.1.call-update) | async-done | bytes 2097168 | tf_op jit(solution)/shard_map/all_gather | solution.py:77
  655.3 6.8 fusion.9
  662.1 5.9 fusion.43
  668.0 73.2 %reduce-scatter.8.cloned.1.call-done = f32[8,256,16]{1,2,0:T(8,128)} async-done(((f32[8,256,256]{1,2,0:T(8,128)}), f32[8,256,16]{1,2,0:T(8,128)}) %reduce-scatter.8.cloned.1.call-update) | async-done | bytes 131088 | tf_op jit(solution)/shard_map/reduce_scatter | solution.py:78
  741.3 1.6 fusion.49
  742.9 65.8 %psum.47 = f32[]{:T(128)} all-reduce(f32[]{:T(128)} %fusion.49), channel_id=1, replica_groups=mesh['row'=8,'col'=16] {'row','col'}, use_global_device_ids=true, to_apply=%region_23.24 | all-reduce | flops 1 | bytes 8 | tf_op jit(solution)/shard_map/psum | solution.py:82
  812.0 0.8 divide_multiply_fusion
  (72 shorter events, 2.5 us)
Async XLA Ops:
  7.2 1.7 copy-start
  21.1 6.4 copy-start.7
  21.1 6.9 copy-start.10
  21.1 7.0 copy-start.11
  21.1 7.1 copy-start.9
  21.1 7.5 copy-start.4
  21.1 8.3 %copy-start.8 = (s32[8,2]{0,1:T(2,128)S(1)}, s32[8,2]{0,1:T(2,128)}, u32[]{:S(2)}) copy-start(s32[8,2]{0,1:T(2,128)} %param.13) | copy-start | bytes 196
  21.1 100.3 %all-to-all-start = ((f32[16,2,256,256]{3,2,1,0:T(8,128)}), f32[16,2,256,256]{3,2,1,0:T(8,128)}, u32[]{:S(2)}, u32[]{:S(2)}) async-start(f32[16,2,256,256]{3,2,1,0:T(8,128)} %select_multiply_fusion), calls=%async_computation | async-start | bytes 16777216 | tf_op jit(solution)/shard_map/all_to_all | solution.py:56
  27.5 100.0 %all-gather.4.cloned.1.call-start = ((), (), s32[]{:S(2)}) async-start(), calls=%async_computation.4 | async-start | bytes 2228224 | tf_op jit(solution)/shard_map/all_gather | solution.py:77
  29.3 184.6 %reduce-scatter.4.cloned.1.call-start = ((), (), s32[]{:S(2)}) async-start(), calls=%async_computation.5 | async-start | bytes 2228224 | tf_op jit(solution)/shard_map/reduce_scatter | solution.py:78
  127.6 6.8 copy-start.1
  140.3 251.4 %all-gather.6.cloned.1.call-start = ((), (), s32[]{:S(2)}) async-start(), calls=%async_computation.6 | async-start | bytes 2228224 | tf_op jit(solution)/shard_map/all_gather | solution.py:77
  350.2 127.4 %reduce-scatter.6.cloned.1.call-start = ((), (), s32[]{:S(2)}) async-start(), calls=%async_computation.7 | async-start | bytes 2228224 | tf_op jit(solution)/shard_map/reduce_scatter | solution.py:78
  391.6 6.8 copy-start.2
  398.4 79.2 %copy-start.5 = (f32[8,256,16]{1,2,0:T(8,128)S(1)}, f32[8,256,16]{1,2,0:T(8,128)}, u32[]{:S(2)}) copy-start(f32[8,256,16]{1,2,0:T(8,128)} %broadcast_divide_fusion.1) | copy-start | bytes 393220
  398.4 149.9 %copy-start.6 = (f32[8,256,16]{1,2,0:T(8,128)S(1)}, f32[8,256,16]{1,2,0:T(8,128)}, u32[]{:S(2)}) copy-start(f32[8,256,16]{1,2,0:T(8,128)} %reduce-scatter.4.cloned.1.call-done) | copy-start | bytes 393220
  404.4 251.0 %all-gather.8.cloned.1.call-start = ((), (), s32[]{:S(2)}) async-start(), calls=%async_computation.8 | async-start | bytes 2228224 | tf_op jit(solution)/shard_map/all_gather | solution.py:77
  613.9 127.4 %reduce-scatter.8.cloned.1.call-start = ((), (), s32[]{:S(2)}) async-start(), calls=%async_computation.9 | async-start | bytes 2228224 | tf_op jit(solution)/shard_map/reduce_scatter | solution.py:78
  655.3 6.8 copy-start.3
Sparse Core Ops, SparseCore 0:
  31.1 46.3 all-gather.3
  140.4 73.5 reduce-scatter.3
  350.3 41.2 all-gather.5
  404.5 73.0 reduce-scatter.5
  614.0 41.2 all-gather.7
  668.2 73.0 reduce-scatter.7
where the time goes:
time: 822 us; the launch traced here: 821 us
  waiting for transfers between devices  390 us (47%)
  blocking collectives  323 us (39%)
  matrix products  38 us (5%)
  between operations  25.5 us (3%)
  other arithmetic  21.1 us (3%)
  local copies, waits for them, and re-layouts  17.1 us (2%)
    psum x5, blocking collectives, combine(): reduced = lax.psum(values, ('row', 'col'))  323 us
    reduce_scatter x3, waiting for transfers between devices, operate(): lax.psum_scatter(contract(full_vector), 'col', scatter_dimension=2, tiled...  220 us
    all_to_all x1, waiting for transfers between devices, local(): lax.all_to_all(outgoing, 'row', split_axis=0, concat_axis=0, tiled=True)  86.8 us
    all_gather x3, waiting for transfers between devices, operate(): full_vector = lax.all_gather(vector, 'col', axis=2, tiled=True)  82.6 us
    dot_general x3, matrix products, contract(): jnp.einsum('swia,sab->swib', left_pick, full_vector, precision=highest)  20.3 us
    dot_general x3, matrix products, contract(): return jnp.einsum('swib,swjb->sij', middle, right_pick, precision=highest)  17.6 us
  transfers between devices with their start and end apart: 7, of which 6 were waited for; matrix products, arithmetic and copies ran while one was open for 2% of the time, Pallas kernels for 0%

commit v1 on v0

--- a/solution.py
+++ b/solution.py
@@ -79,7 +79,8 @@
         return total_sum * start_mask
 
     def combine(values):
-        reduced = lax.psum(values, ("row", "col"))
+        inner = lax.psum(values, "col")
+        reduced = lax.psum(inner, "row")
         return reduced
 
     image_vec = operate(start_vec)

time: 822 us -> 754 us (0.917)
  blocking collectives: 323 us -> 259 us
    psum x5 -> x10, blocking collectives: 323 us -> 259 us  [the longest x5 153 us: combine(): inner = lax.psum(values, 'col')]
where the time goes in v1:
time: 754 us; the launch traced here: 753 us
  waiting for transfers between devices  386 us (51%)
  blocking collectives  259 us (34%)
  matrix products  38 us (5%)
  between operations  25.5 us (3%)
  other arithmetic  21.1 us (3%)
  local copies, waits for them, and re-layouts  17.1 us (2%)
    reduce_scatter x3, waiting for transfers between devices, operate(): lax.psum_scatter(contract(full_vector), 'col', scatter_dimension=2, tiled...  220 us
    psum x5, blocking collectives, combine(): inner = lax.psum(values, 'col')  153 us
    psum x5, blocking collectives, combine(): reduced = lax.psum(inner, 'row')  106 us
    all_to_all x1, waiting for transfers between devices, local(): lax.all_to_all(outgoing, 'row', split_axis=0, concat_axis=0, tiled=True)  86.8 us
    all_gather x3, waiting for transfers between devices, operate(): full_vector = lax.all_gather(vector, 'col', axis=2, tiled=True)  78.7 us
    dot_general x3, matrix products, contract(): jnp.einsum('swia,sab->swib', left_pick, full_vector, precision=highest)  20.3 us
    dot_general x3, matrix products, contract(): return jnp.einsum('swib,swjb->sij', middle, right_pick, precision=highest)  17.6 us
  transfers between devices with their start and end apart: 7, of which 6 were waited for; matrix products, arithmetic and copies ran while one was open for 2% of the time, Pallas kernels for 0%

profile of v1, /device:TPU:1, one launch (start us, length us, event | category | flops | bytes accessed | tf_op | source)
XLA Modules:
  0.0 752.9 jit_solution(632695455833942023)
XLA Ops:
  8.9 4.3 gather_fusion
  13.2 7.9 %select_multiply_fusion = f32[16,2,256,256]{3,2,1,0:T(8,128)} fusion(f32[16,2,256,256]{3,2,1,0:T(8,128)} %gather_fusion, f32[16]{0:T(128)S(1)} %reshape.149, pred[16]{0:T(512)(128)(4,1)S(1)} %compare_and_fusion.1), kind=kLoop, calls=%fused_computation.3 | loop fusion | flops 4194304 | bytes 16777296 | tf_op jit(solution)/shard_map/mul | solution.py:54
  21.1 6.4 all-to-all-start
  29.5 4.9 gather_fusion.2
  34.5 86.8 %all-to-all-done = f32[16,2,256,256]{3,2,1,0:T(8,128)} async-done(((f32[16,2,256,256]{3,2,1,0:T(8,128)}), f32[16,2,256,256]{3,2,1,0:T(8,128)}, u32[]{:S(2)}, u32[]{:S(2)}) %all-to-all-start) | async-done | bytes 8388640 | tf_op jit(solution)/shard_map/all_to_all | solution.py:56
  121.4 6.2 gather_fusion.1
  127.6 6.8 fusion.13
  134.4 5.9 fusion.33
  140.3 73.6 %reduce-scatter.4.cloned.1.call-done = f32[8,256,16]{1,2,0:T(8,128)} async-done(((f32[8,256,256]{1,2,0:T(8,128)}), f32[8,256,16]{1,2,0:T(8,128)}) %reduce-scatter.4.cloned.1.call-update) | async-done | bytes 131088 | tf_op jit(solution)/shard_map/reduce_scatter | solution.py:78
  213.9 1.6 multiply_reduce_fusion.4
  215.6 31.5 %all-reduce = (f32[]{:T(128)}, f32[]{:T(128)}) all-reduce(f32[]{:T(128)} %get-tuple-element.3, f32[]{:T(128)} %get-tuple-element.2), channel_id=1, replica_groups=mesh['row'=8,'col'=16] {'col'}, use_global_device_ids=true, to_apply=%region_14.15 | all-reduce | flops 2 | bytes 16 | tf_op jit(solution)/shard_map/psum | solution.py:82
  247.0 22.0 %all-reduce.1 = (f32[]{:T(128)}, f32[]{:T(128)}) all-reduce(f32[]{:T(128)} %get-tuple-element.6, f32[]{:T(128)} %get-tuple-element.7), channel_id=1, replica_groups=mesh['row'=8,'col'=16] {'row'}, use_global_device_ids=true, to_apply=%region_15.16 | all-reduce | flops 2 | bytes 16 | tf_op jit(solution)/shard_map/psum | solution.py:83
  271.0 1.6 multiply_reduce_fusion.2
  272.6 29.1 %psum.88 = f32[]{:T(128)} all-reduce(f32[]{:T(128)} %multiply_reduce_fusion.2), channel_id=1, replica_groups=mesh['row'=8,'col'=16] {'col'}, use_global_device_ids=true, to_apply=%region_17.18 | all-reduce | flops 1 | bytes 8 | tf_op jit(solution)/shard_map/psum | solution.py:82
  301.8 20.0 %psum.89 = f32[]{:T(128)} all-reduce(f32[]{:T(128)} %psum.88), channel_id=1, replica_groups=mesh['row'=8,'col'=16] {'row'}, use_global_device_ids=true, to_apply=%region_18.19 | all-reduce | flops 1 | bytes 8 | tf_op jit(solution)/shard_map/psum | solution.py:83
  322.4 1.7 broadcast_divide_fusion.1
  324.4 39.4 %all-gather.6.cloned.1.call-done = f32[8,256,256]{1,2,0:T(8,128)} async-done(((f32[8,256,16]{1,2,0:T(8,128)}), f32[8,256,256]{1,2,0:T(8,128)}) %all-gather.6.cloned.1.call-update) | async-done | bytes 2097168 | tf_op jit(solution)/shard_map/all_gather | solution.py:77
  363.7 6.8 fusion.11
  370.6 5.9 fusion.38
  376.5 73.2 %reduce-scatter.6.cloned.1.call-done = f32[8,256,16]{1,2,0:T(8,128)} async-done(((f32[8,256,256]{1,2,0:T(8,128)}), f32[8,256,16]{1,2,0:T(8,128)}) %reduce-scatter.6.cloned.1.call-update) | async-done | bytes 131088 | tf_op jit(solution)/shard_map/reduce_scatter | solution.py:78
  449.7 1.6 multiply_reduce_fusion.1
  451.3 31.5 %psum.90 = f32[]{:T(128)} all-reduce(f32[]{:T(128)} %multiply_reduce_fusion.1), channel_id=1, replica_groups=mesh['row'=8,'col'=16] {'col'}, use_global_device_ids=true, to_apply=%region_21.22 | all-reduce | flops 1 | bytes 8 | tf_op jit(solution)/shard_map/psum | solution.py:82
  482.8 21.9 %psum.91 = f32[]{:T(128)} all-reduce(f32[]{:T(128)} %psum.90), channel_id=1, replica_groups=mesh['row'=8,'col'=16] {'row'}, use_global_device_ids=true, to_apply=%region_22.23 | all-reduce | flops 1 | bytes 8 | tf_op jit(solution)/shard_map/psum | solution.py:83
  508.1 1.7 multiply_reduce_fusion
  509.7 29.1 %psum.92 = f32[]{:T(128)} all-reduce(f32[]{:T(128)} %get-tuple-element.10), channel_id=1, replica_groups=mesh['row'=8,'col'=16] {'col'}, use_global_device_ids=true, to_apply=%region_24.25 | all-reduce | flops 1 | bytes 8 | tf_op jit(solution)/shard_map/psum | solution.py:82
  538.8 20.1 %psum.93 = f32[]{:T(128)} all-reduce(f32[]{:T(128)} %psum.92), channel_id=1, replica_groups=mesh['row'=8,'col'=16] {'row'}, use_global_device_ids=true, to_apply=%region_25.26 | all-reduce | flops 1 | bytes 8 | tf_op jit(solution)/shard_map/psum | solution.py:83
  560.5 39.3 %all-gather.8.cloned.1.call-done = f32[8,256,256]{1,2,0:T(8,128)} async-done(((f32[8,256,16]{1,2,0:T(8,128)}), f32[8,256,256]{1,2,0:T(8,128)}) %all-gather.8.cloned.1.call-update) | async-done | bytes 2097168 | tf_op jit(solution)/shard_map/all_gather | solution.py:77
  599.9 6.8 fusion.9
  606.7 5.9 fusion.43
  612.6 73.3 %reduce-scatter.8.cloned.1.call-done = f32[8,256,16]{1,2,0:T(8,128)} async-done(((f32[8,256,256]{1,2,0:T(8,128)}), f32[8,256,16]{1,2,0:T(8,128)}) %reduce-scatter.8.cloned.1.call-update) | async-done | bytes 131088 | tf_op jit(solution)/shard_map/reduce_scatter | solution.py:78
  687.5 31.5 %psum.94 = f32[]{:T(128)} all-reduce(f32[]{:T(128)} %fusion.49), channel_id=1, replica_groups=mesh['row'=8,'col'=16] {'col'}, use_global_device_ids=true, to_apply=%region_28.29 | all-reduce | flops 1 | bytes 8 | tf_op jit(solution)/shard_map/psum | solution.py:82
  719.0 21.9 %psum.95 = f32[]{:T(128)} all-reduce(f32[]{:T(128)} %psum.94), channel_id=1, replica_groups=mesh['row'=8,'col'=16] {'row'}, use_global_device_ids=true, to_apply=%region_29.30 | all-reduce | flops 1 | bytes 8 | tf_op jit(solution)/shard_map/psum | solution.py:83
  (77 shorter events, 7.4 us)
Async XLA Ops:
  7.2 1.7 copy-start
  21.1 6.4 copy-start.7
  21.1 6.9 copy-start.10
  21.1 7.0 copy-start.11
  21.1 7.1 copy-start.9
  21.1 7.5 copy-start.4
  21.1 8.3 %copy-start.8 = (s32[8,2]{0,1:T(2,128)S(1)}, s32[8,2]{0,1:T(2,128)}, u32[]{:S(2)}) copy-start(s32[8,2]{0,1:T(2,128)} %param.13) | copy-start | bytes 196
  21.1 100.3 %all-to-all-start = ((f32[16,2,256,256]{3,2,1,0:T(8,128)}), f32[16,2,256,256]{3,2,1,0:T(8,128)}, u32[]{:S(2)}, u32[]{:S(2)}) async-start(f32[16,2,256,256]{3,2,1,0:T(8,128)} %select_multiply_fusion), calls=%async_computation | async-start | bytes 16777216 | tf_op jit(solution)/shard_map/all_to_all | solution.py:56
  27.5 100.0 %all-gather.4.cloned.1.call-start = ((), (), s32[]{:S(2)}) async-start(), calls=%async_computation.4 | async-start | bytes 2228224 | tf_op jit(solution)/shard_map/all_gather | solution.py:77
  29.3 184.6 %reduce-scatter.4.cloned.1.call-start = ((), (), s32[]{:S(2)}) async-start(), calls=%async_computation.5 | async-start | bytes 2228224 | tf_op jit(solution)/shard_map/reduce_scatter | solution.py:78
  127.6 6.8 copy-start.1
  140.3 223.5 %all-gather.6.cloned.1.call-start = ((), (), s32[]{:S(2)}) async-start(), calls=%async_computation.6 | async-start | bytes 2228224 | tf_op jit(solution)/shard_map/all_gather | solution.py:77
  324.1 125.5 %reduce-scatter.6.cloned.1.call-start = ((), (), s32[]{:S(2)}) async-start(), calls=%async_computation.7 | async-start | bytes 2228224 | tf_op jit(solution)/shard_map/reduce_scatter | solution.py:78
  363.7 6.8 copy-start.2
  370.5 79.2 %copy-start.5 = (f32[8,256,16]{1,2,0:T(8,128)S(1)}, f32[8,256,16]{1,2,0:T(8,128)}, u32[]{:S(2)}) copy-start(f32[8,256,16]{1,2,0:T(8,128)} %broadcast_divide_fusion.1) | copy-start | bytes 393220
  370.5 137.5 %copy-start.6 = (f32[8,256,16]{1,2,0:T(8,128)S(1)}, f32[8,256,16]{1,2,0:T(8,128)}, u32[]{:S(2)}) copy-start(f32[8,256,16]{1,2,0:T(8,128)} %reduce-scatter.4.cloned.1.call-done) | copy-start | bytes 393220
  376.5 223.4 %all-gather.8.cloned.1.call-start = ((), (), s32[]{:S(2)}) async-start(), calls=%async_computation.8 | async-start | bytes 2228224 | tf_op jit(solution)/shard_map/all_gather | solution.py:77
  560.3 125.6 %reduce-scatter.8.cloned.1.call-start = ((), (), s32[]{:S(2)}) async-start(), calls=%async_computation.9 | async-start | bytes 2228224 | tf_op jit(solution)/shard_map/reduce_scatter | solution.py:78
  599.9 6.8 copy-start.3
Sparse Core Ops, SparseCore 0:
  31.1 46.3 all-gather.3
  140.4 73.5 reduce-scatter.3
  324.3 39.4 all-gather.5
  376.6 73.0 reduce-scatter.5
  560.4 39.4 all-gather.7
  612.7 73.1 reduce-scatter.7
